TPU v7x, 512 devices: a whole 4x4x16 slice. The times are simulated.
512 devices in a mesh: seq: 8 (over x, core), tok: 64 (over z, y).
Axes of the slice: x: 4, y: 4, z: 16, core: 2. Of those that a mesh axis runs over, the one named last changes fastest.
Arguments:
- block_in: bfloat16 [8, 256, 1024], P('seq'), may hold values from -6 to 6
- accept: int32 [2, 8, 256], P(None, 'seq'), may hold values 0 or 1
- cache_len: int32 [8], P('seq'), may hold values from 8192 to 16384, as said below
- slot_page: int32 [8, 192], P('seq', 'tok'), may hold values from -1 to 127, as said below
- cache_kv: bfloat16 [8, 192, 128, 2048], P('seq', 'tok'), as said below
- w_query: bfloat16 [1024, 1024], P('seq', 'tok'), may hold values from -0.25 to 0.25
- w_key_value: bfloat16 [1024, 2048], P('seq', 'tok'), may hold values from -0.375 to 0.375
- w_out: bfloat16 [1024, 1024], P('seq', 'tok'), may hold values from -0.1875 to 0.1875
- gain_attn: float32 [1024], replicated, may hold values from 0.1 to 1.9
- w_up: bfloat16 [1024, 4096], P('seq', 'tok'), may hold values from -0.1875 to 0.1875
- w_down: bfloat16 [4096, 1024], P('tok', 'seq'), may hold values from -0.09375 to 0.09375
- gain_mlp: float32 [1024], replicated, may hold values from 0.1 to 1.9
Outputs:
- refined: bfloat16 [8, 256, 1024], P('seq')
Inputs may be any that keep to these rules, and one draw needn't show every extreme that they name: `cache_len`: one sequence has exactly 16384 cached tokens. `slot_page`: slots j * 3 to (j + 1) * 3 - 1 of a row are those of index j of tok. Each page 0 to ceil(cache_len[s] / 128) - 1 of sequence s is in exactly one slot of row s, every other slot holds -1, and in every row some index of tok has all 3 of its slots filled. `cache_kv`: finite values; entries of empty slots are arbitrary.
All inputs are finite; a program needn't handle non-finite values. No bound on the sum of `accept` on one device may be relied on, other than what follows from the above.
Results may differ from a plain program's by a relative error of at most 0.035.
The roundings to bfloat16 on the way count: a program that leaves them out, or rounds other values in their place, can miss the bound.
Values may be sent and summed in bfloat16 or wider, within the bound.
A program may use at most 64 MiB of HBM per device.

v0:
```python
import jax
import jax.numpy as jnp
from jax import lax
from jax.sharding import PartitionSpec as P

HEADS = 16
HEAD_DIM = 64
EPSILON = 1e-05
FLOOR_SCORE = -1e30


def layer_norm(values, gain_vec):
    average = jnp.mean(values, axis=-1, keepdims=True)
    centered = values - average
    variance = jnp.mean(centered * centered, axis=-1, keepdims=True)
    return centered * lax.rsqrt(variance + EPSILON) * gain_vec


def merge_state(earlier, later):
    overall = jnp.maximum(earlier[0], later[0])
    early_factor = jnp.exp(earlier[0] - overall)
    late_factor = jnp.exp(later[0] - overall)
    totals = earlier[1] * early_factor + later[1] * late_factor
    weighted = earlier[2] * early_factor[..., None] + later[2] * late_factor[..., None]
    return (overall, totals, weighted)


def page_partial(queries, page_keys, page_values, usable):
    scores = jnp.einsum(
        "sqhe,skhe->sqhk", queries, page_keys, preferred_element_type=jnp.float32
    ) * HEAD_DIM ** (-0.5)
    masked = jnp.where(usable[:, None, None, :], scores, FLOOR_SCORE)
    peaks = jnp.max(masked, axis=-1)
    weights = jnp.where(usable[:, None, None, :], jnp.exp(masked - peaks[..., None]), 0.0).astype(
        jnp.bfloat16
    )
    weighted = jnp.einsum(
        "sqhk,skhe->sqhe", weights, page_values, preferred_element_type=jnp.float32
    )
    totals = jnp.sum(weights.astype(jnp.float32), axis=-1)
    return (peaks, totals, weighted)


def shards(
    block_in,
    accept,
    cache_len,
    slot_page,
    cache_kv,
    w_query,
    w_key_value,
    w_out,
    gain_attn,
    w_up,
    w_down,
    gain_mlp,
):
    groups, block_len, model_width = block_in.shape
    tok_parts = lax.axis_size("tok")
    tok_dev = block_len // tok_parts
    slot_count = cache_kv.shape[1]
    page_len = cache_kv.shape[2]
    own_index = lax.axis_index("tok")
    rows_q, rows_kv, rows_o, rows_up, cols_down = (
        lax.all_gather(w_query, "seq", axis=0, tiled=True),
        lax.all_gather(w_key_value, "seq", axis=0, tiled=True),
        lax.all_gather(w_out, "seq", axis=0, tiled=True),
        lax.all_gather(w_up, "seq", axis=0, tiled=True),
        lax.all_gather(w_down, "seq", axis=1, tiled=True),
    )
    full_q, full_kv, full_o = (
        lax.all_gather(rows_q, "tok", axis=1, tiled=True),
        lax.all_gather(rows_kv, "tok", axis=1, tiled=True),
        lax.all_gather(rows_o, "tok", axis=1, tiled=True),
    )

    def attend(inputs):
        flat_all = inputs.reshape(groups * block_len, model_width)
        own_rows = lax.dynamic_slice_in_dim(inputs, own_index * tok_dev, tok_dev, 1)
        flat_rows = own_rows.reshape(groups * tok_dev, model_width)
        queries = jnp.dot(flat_all, full_q, preferred_element_type=jnp.float32).astype(jnp.bfloat16)
        own_pair = jnp.dot(flat_rows, full_kv, preferred_element_type=jnp.float32).astype(
            jnp.bfloat16
        )
        own_pair = own_pair.reshape(groups, tok_dev, 2 * model_width)
        queries = queries.reshape(groups, block_len, HEADS, HEAD_DIM)
        own_keys = own_pair[..., :model_width].reshape(groups, tok_dev, HEADS, HEAD_DIM)
        own_values = own_pair[..., model_width:].reshape(groups, tok_dev, HEADS, HEAD_DIM)
        carry_state = page_partial(
            queries, own_keys, own_values, jnp.ones((groups, tok_dev), dtype=bool)
        )

        def slot_step(slot_index, carry_state):
            page_pair = lax.dynamic_index_in_dim(cache_kv, slot_index, 1, keepdims=False)
            page_no = lax.dynamic_index_in_dim(slot_page, slot_index, 1, keepdims=False)
            positions = page_no[:, None] * page_len + jnp.arange(page_len, dtype=jnp.int32)[None, :]
            usable = (page_no[:, None] >= 0) & (positions < cache_len[:, None])
            page_keys = page_pair[..., :model_width].reshape(groups, page_len, HEADS, HEAD_DIM)
            page_values = page_pair[..., model_width:].reshape(groups, page_len, HEADS, HEAD_DIM)
            return merge_state(carry_state, page_partial(queries, page_keys, page_values, usable))

        peaks, totals, weighted = lax.fori_loop(0, slot_count, slot_step, carry_state)
        peak_parts = lax.all_to_all(peaks[None], "tok", split_axis=2, concat_axis=0, tiled=True)
        total_parts = lax.all_to_all(totals[None], "tok", split_axis=2, concat_axis=0, tiled=True)
        weighted_parts = lax.all_to_all(
            weighted.reshape(groups, block_len, model_width)[None],
            "tok",
            split_axis=2,
            concat_axis=0,
            tiled=True,
        )
        overall = jnp.max(peak_parts, axis=0)
        factor = jnp.exp(peak_parts - overall[None])
        denominator = jnp.sum(total_parts * factor, axis=0)
        split_parts = weighted_parts.reshape(weighted_parts.shape[:-1] + (HEADS, HEAD_DIM))
        numerator = jnp.sum(split_parts * factor[..., None], axis=0)
        attention = (numerator / denominator[..., None]).reshape(
            numerator.shape[:-2] + (model_width,)
        )
        attention = attention.astype(jnp.bfloat16).reshape(groups * tok_dev, model_width)
        residual = flat_rows.astype(jnp.float32) + jnp.dot(
            attention, full_o, preferred_element_type=jnp.float32
        )
        return (
            layer_norm(residual, gain_attn)
            .astype(jnp.bfloat16)
            .reshape(groups, tok_dev, model_width)
        )

    def feed(settled):
        products = jnp.einsum(
            "gtd,df->gtf",
            lax.all_gather(settled, "tok", axis=1, tiled=True),
            rows_up,
            preferred_element_type=jnp.float32,
        )
        hidden = jax.nn.gelu(products, approximate=False).astype(jnp.bfloat16)
        mlp_term = jnp.einsum("gtf,fd->gtd", hidden, cols_down, preferred_element_type=jnp.float32)
        projected = lax.psum_scatter(mlp_term, "tok", scatter_dimension=1, tiled=True)
        finished = layer_norm(settled.astype(jnp.float32) + projected, gain_mlp).astype(
            jnp.bfloat16
        )
        return lax.all_gather(finished, "tok", axis=1, tiled=True)

    first_out = feed(attend(block_in))
    second_in = jnp.where(accept[0][..., None] == 1, first_out, block_in)
    second_out = feed(attend(second_in))
    return jnp.where(accept[1][..., None] == 1, second_out, second_in)


def solution(mesh):
    in_specs = (
        P("seq", None, None),
        P(None, "seq", None),
        P("seq"),
        P("seq", "tok"),
        P("seq", "tok", None, None),
        P("seq", "tok"),
        P("seq", "tok"),
        P("seq", "tok"),
        P(),
        P("seq", "tok"),
        P("tok", "seq"),
        P(),
    )
    out_specs = P("seq", None, None)
    return jax.shard_map(shards, mesh=mesh, in_specs=in_specs, out_specs=out_specs, check_vma=False)
```

profile of v0, /device:TPU:2, one launch (start us, length us, event | category | flops | bytes accessed | tf_op | source)
XLA Modules:
  0.0 1601.0 jit_solution(3491275169055620532)
XLA Ops:
  6.5 16.2 %all_gather.38 = bf16[1024,16]{0,1:T(8,128)(2,1)} all-gather(bf16[128,16]{0,1:T(8,128)(2,1)} %param.21), channel_id=1, replica_groups=mesh['seq'=8,'tok'=64] {'seq'}, dimensions={0}, use_global_device_ids=true | all-gather | bytes 36864 | tf_op jit(solution)/shard_map/all_gather | solution.py:65
  22.9 13.1 all_gather.36
  38.0 126.6 %all-gather.10.cloned.1.call-done = bf16[1024,1024]{0,1:T(8,128)(2,1)} async-done(((bf16[1024,16]{0,1:T(8,128)(2,1)}), bf16[1024,1024]{0,1:T(8,128)(2,1)}) %all-gather.10.cloned.1.call-update) | async-done | bytes 2097168 | tf_op jit(solution)/shard_map/all_gather | solution.py:72
  167.1 143.0 %all-gather.8.cloned.1.call-done = bf16[1024,2048]{0,1:T(8,128)(2,1)} async-done(((bf16[1024,32]{0,1:T(8,128)(2,1)}), bf16[1024,2048]{0,1:T(8,128)(2,1)}) %all-gather.8.cloned.1.call-update) | async-done | bytes 4194320 | tf_op jit(solution)/shard_map/all_gather | solution.py:73
  310.1 3.4 fusion.32
  314.3 14.3 while.34
  329.3 8.9 all-to-all-start.1
  339.0 15.4 all-to-all-done.1
  354.4 4.6 all-to-all-start.2
  361.0 14.3 all-to-all-done.2
  375.3 5.5 all-to-all-start
  380.9 12.7 all_gather.40
  393.6 11.0 all_gather.43
  404.6 11.2 all_gather.44
  420.9 4.6 all-to-all-done
  425.5 3.1 multiply_reduce_fusion.1
  428.6 106.4 %all-gather.12.cloned.1.call-done = bf16[1024,1024]{0,1:T(8,128)(2,1)} async-done(((bf16[1024,16]{0,1:T(8,128)(2,1)}), bf16[1024,1024]{0,1:T(8,128)(2,1)}) %all-gather.12.cloned.1.call-update) | async-done | bytes 2097168 | tf_op jit(solution)/shard_map/all_gather | solution.py:74
  537.6 98.1 %all-gather.2 = bf16[64,4,1024]{2,1,0:T(4,128)(2,1)S(1)} all-gather(bf16[1,4,1024]{2,1,0:T(4,128)(2,1)S(1)} %fusion.126), channel_id=2, replica_groups=mesh['seq'=8,'tok'=64] {'tok'}, dimensions={0}, use_global_device_ids=true | all-gather | bytes 532480 | tf_op jit(solution)/shard_map/all_gather | solution.py:133
  636.7 3.0 convolution_bitcast_fusion.4
  641.7 266.9 %all-reduce.5.cloned.1.call-done = f32[1,256,1024]{2,1,0:T(8,128)} async-done(((f32[1,256,1024]{2,1,0:T(8,128)}), f32[1,256,1024]{2,1,0:T(8,128)}) %all-reduce.5.cloned.1.call-update) | async-done | bytes 1048592
  911.5 98.7 %all_gather.45 = bf16[1,256,1024]{2,0,1:T(2,128)(2,1)S(1)} all-gather(bf16[1,4,1024]{2,0,1:T(2,128)(2,1)S(1)} %copy.77), channel_id=1, replica_groups=mesh['seq'=8,'tok'=64] {'tok'}, dimensions={1}, use_global_device_ids=true | all-gather | bytes 532480 | tf_op jit(solution)/shard_map/all_gather | solution.py:143
  1011.5 3.4 fusion.33
  1015.7 14.5 while.35
  1030.9 10.5 all-to-all-start.4
  1042.2 15.4 all-to-all-done.4
  1057.6 5.9 all-to-all-start.5
  1065.5 16.6 %all-to-all-done.5 = f32[1,1,256,16]{3,1,0,2:T(1,128)S(1)} async-done(((f32[1,1,256,16]{3,1,0,2:T(1,128)}), f32[1,1,256,16]{3,1,0,2:T(1,128)S(1)}, u32[]{:S(2)}, u32[]{:S(2)}) %all-to-all-start.5) | async-done | bytes 16416 | tf_op jit(solution)/shard_map/all_to_all | solution.py:104
  1082.1 5.0 all-to-all-start.3
  1092.5 28.2 %all-to-all-done.3 = f32[1,1,256,1024]{3,1,0,2:T(1,128)S(1)} async-done(((f32[1,1,256,1024]{3,1,0,2:T(1,128)}), f32[1,1,256,1024]{3,1,0,2:T(1,128)S(1)}, u32[]{:S(2)}, u32[]{:S(2)}) %all-to-all-start.3) | async-done | bytes 1048608 | tf_op jit(solution)/shard_map/all_to_all | solution.py:105
  1125.4 99.8 %all-gather.3 = bf16[64,4,1024]{2,1,0:T(4,128)(2,1)S(1)} all-gather(bf16[1,4,1024]{2,1,0:T(4,128)(2,1)S(1)} %fusion.127), channel_id=3, replica_groups=mesh['seq'=8,'tok'=64] {'tok'}, dimensions={0}, use_global_device_ids=true | all-gather | bytes 532480 | tf_op jit(solution)/shard_map/all_gather | solution.py:133
  1227.3 265.2 %all-reduce.7.cloned.1.call-done = f32[1,256,1024]{2,1,0:T(8,128)} async-done(((f32[1,256,1024]{2,1,0:T(8,128)}), f32[1,256,1024]{2,1,0:T(8,128)}) %all-reduce.7.cloned.1.call-update) | async-done | bytes 1048592
  1495.3 98.1 %all_gather.47 = bf16[1,256,1024]{2,0,1:T(2,128)(2,1)S(1)} all-gather(bf16[1,4,1024]{2,0,1:T(2,128)(2,1)S(1)} %copy.87), channel_id=1, replica_groups=mesh['seq'=8,'tok'=64] {'tok'}, dimensions={1}, use_global_device_ids=true | all-gather | bytes 532480 | tf_op jit(solution)/shard_map/all_gather | solution.py:143
  (163 shorter events, 68.0 us)
Async XLA Ops:
  6.5 158.0 %copy-start.2 = (bf16[1,256,1024]{2,1,0:T(8,128)(2,1)S(1)}, bf16[1,256,1024]{2,1,0:T(8,128)(2,1)}, u32[]{:S(2)}) copy-start(bf16[1,256,1024]{2,1,0:T(8,128)(2,1)} %param.16) | copy-start | bytes 1572868
  6.5 158.0 %all-gather.10.cloned.1.call-start = ((), (), s32[]{:S(2)}) async-start(), calls=%async_computation.7 | async-start | bytes 2129920 | tf_op jit(solution)/shard_map/all_gather | solution.py:72
  22.8 287.3 %all-gather.8.cloned.1.call-start = ((), (), s32[]{:S(2)}) async-start(), calls=%async_computation.6 | async-start | bytes 4259840 | tf_op jit(solution)/shard_map/all_gather | solution.py:73
  167.1 147.2 %copy-start.5 = (s32[1,3]{1,0:T(1,128)S(1)}, s32[1,3]{1,0:T(1,128)}, u32[]{:S(2)}) copy-start(s32[1,3]{1,0:T(1,128)} %param.19) | copy-start | bytes 40
  329.3 25.0 %all-to-all-start.1 = ((f32[1,1,256,16]{3,1,0,2:T(1,128)}), f32[1,1,256,16]{3,1,0,2:T(1,128)S(1)}, u32[]{:S(2)}, u32[]{:S(2)}) async-start(f32[1,1,256,16]{3,1,0,2:T(1,128)} %bitcast.47), calls=%async_computation.1 | async-start | bytes 262144 | tf_op jit(solution)/shard_map/all_to_all | solution.py:103
  354.4 20.9 %all-to-all-start.2 = ((f32[1,1,256,16]{3,1,0,2:T(1,128)}), f32[1,1,256,16]{3,1,0,2:T(1,128)S(1)}, u32[]{:S(2)}, u32[]{:S(2)}) async-start(f32[1,1,256,16]{3,1,0,2:T(1,128)} %bitcast.49), calls=%async_computation.2 | async-start | bytes 262144 | tf_op jit(solution)/shard_map/all_to_all | solution.py:104
  359.0 21.9 %copy-start.9 = (bf16[128,16]{0,1:T(8,128)(2,1)S(1)}, bf16[128,16]{0,1:T(8,128)(2,1)}, u32[]{:S(2)}) copy-start(bf16[128,16]{0,1:T(8,128)(2,1)} %param.23) | copy-start | bytes 12292
  359.0 34.6 %copy-start.6 = (bf16[128,64]{0,1:T(8,128)(2,1)S(1)}, bf16[128,64]{0,1:T(8,128)(2,1)}, u32[]{:S(2)}) copy-start(bf16[128,64]{0,1:T(8,128)(2,1)} %param.25) | copy-start | bytes 49156
  359.0 45.6 %copy-start.7 = (bf16[64,128]{1,0:T(8,128)(2,1)S(1)}, bf16[64,128]{1,0:T(8,128)(2,1)}, u32[]{:S(2)}) copy-start(bf16[64,128]{1,0:T(8,128)(2,1)} %param.26) | copy-start | bytes 49156
  375.3 50.2 %all-to-all-start = ((f32[1,1,256,1024]{3,1,0,2:T(1,128)}), f32[1,1,256,1024]{3,1,0,2:T(1,128)}, u32[]{:S(2)}, u32[]{:S(2)}) async-start(f32[1,1,256,1024]{3,1,0,2:T(1,128)} %copy.74), calls=%async_computation | async-start | bytes 2097152 | tf_op jit(solution)/shard_map/all_to_all | solution.py:105
  380.8 154.2 %all-gather.12.cloned.1.call-start = ((), (), s32[]{:S(2)}) async-start(), calls=%async_computation.8 | async-start | bytes 2129920 | tf_op jit(solution)/shard_map/all_gather | solution.py:74
  393.5 515.0 %all-reduce.5.cloned.1.call-start = ((), (), s32[]{:S(2)}) async-start(), calls=%async_computation.9 | async-start | bytes 2097152
  418.2 116.8 %copy-start.3 = (bf16[1,256,1024]{2,1,0:T(8,128)(2,1)S(1)}, bf16[1,256,1024]{2,1,0:T(8,128)(2,1)}, u32[]{:S(2)}) copy-start(bf16[1,256,1024]{2,1,0:T(8,128)(2,1)} %param.16) | copy-start | bytes 1572868
  425.5 112.1 %copy-start.4 = (f32[1024]{0:T(1024)S(1)}, f32[1024]{0:T(1024)}, u32[]{:S(2)}) copy-start(f32[1024]{0:T(1024)} %param.24) | copy-start | bytes 12292
  635.8 5.9 copy-start.10
  635.8 274.8 %copy-start.8 = (f32[1024]{0:T(1024)S(1)}, f32[1024]{0:T(1024)}, u32[]{:S(2)}) copy-start(f32[1024]{0:T(1024)} %param.27) | copy-start | bytes 12292
  908.5 101.9 %copy-start.11 = (bf16[1024,1024]{0,1:T(8,128)(2,1)S(1)}, bf16[1024,1024]{0,1:T(8,128)(2,1)}, u32[]{:S(2)}) copy-start(bf16[1024,1024]{0,1:T(8,128)(2,1)} %all-gather.10.cloned.1.call-done) | copy-start | bytes 6291460
  1010.4 1.0 copy-start
  1030.9 26.7 %all-to-all-start.4 = ((f32[1,1,256,16]{3,1,0,2:T(1,128)}), f32[1,1,256,16]{3,1,0,2:T(1,128)S(1)}, u32[]{:S(2)}, u32[]{:S(2)}) async-start(f32[1,1,256,16]{3,1,0,2:T(1,128)} %bitcast.70), calls=%async_computation.4 | async-start | bytes 262144 | tf_op jit(solution)/shard_map/all_to_all | solution.py:103
  1057.6 24.5 %all-to-all-start.5 = ((f32[1,1,256,16]{3,1,0,2:T(1,128)}), f32[1,1,256,16]{3,1,0,2:T(1,128)S(1)}, u32[]{:S(2)}, u32[]{:S(2)}) async-start(f32[1,1,256,16]{3,1,0,2:T(1,128)} %bitcast.72), calls=%async_computation.5 | async-start | bytes 262144 | tf_op jit(solution)/shard_map/all_to_all | solution.py:104
  1082.1 38.6 %all-to-all-start.3 = ((f32[1,1,256,1024]{3,1,0,2:T(1,128)}), f32[1,1,256,1024]{3,1,0,2:T(1,128)S(1)}, u32[]{:S(2)}, u32[]{:S(2)}) async-start(f32[1,1,256,1024]{3,1,0,2:T(1,128)} %copy.84), calls=%async_computation.3 | async-start | bytes 2097152 | tf_op jit(solution)/shard_map/all_to_all | solution.py:105
  1087.1 405.4 %all-reduce.7.cloned.1.call-start = ((), (), s32[]{:S(2)}) async-start(), calls=%async_computation.10 | async-start | bytes 2097152
  1089.8 33.0 %copy-start.1 = (bf16[1,256,1024]{2,1,0:T(8,128)(2,1)S(1)}, bf16[1,256,1024]{2,1,0:T(8,128)(2,1)}, u32[]{:S(2)}) copy-start(bf16[1,256,1024]{2,1,0:T(8,128)(2,1)} %copy-done) | copy-start | bytes 1572868
Sparse Core Ops, SparseCore 0:
  22.9 141.5 all-gather.9
  167.5 142.5 all-gather.7
  393.7 141.2 all-gather.11
  639.8 268.6 all-reduce.4
  1227.5 265.0 all-reduce.6
where the time goes:
time: 1600 us
  waiting for transfers between devices  1000 us (62%)
  blocking collectives  459 us (29%)
  starting transfers between devices  40.8 us (3%)
  matrix products  29.6 us (2%)
  other arithmetic  28.5 us (2%)
  local copies, waits for them, and re-layouts  22.3 us (1%)
    unnamed x7, waiting for transfers between devices  532 us
    all_gather x2, blocking collectives, feed(): lax.all_gather(settled, 'tok', axis=1, tiled=True)  198 us
    all_gather x2, blocking collectives, feed(): return lax.all_gather(finished, 'tok', axis=1, tiled=True)  197 us
    all_gather x1, waiting for transfers between devices, shards(): lax.all_gather(rows_kv, 'tok', axis=1, tiled=True)  143 us
    all_gather x1, waiting for transfers between devices, shards(): lax.all_gather(rows_q, 'tok', axis=1, tiled=True)  127 us
    all_gather x1, waiting for transfers between devices, shards(): lax.all_gather(rows_o, 'tok', axis=1, tiled=True)  106 us
    all_to_all x2, waiting for transfers between devices, attend(): lax.all_to_all(weighted.reshape(groups, block_len, model_width)[None], 't...  32.7 us
  transfers between devices with their start and end apart: 11, of which 11 were waited for; matrix products, arithmetic and copies ran while one was open for 2% of the time, Pallas kernels for 0%

commit v1 on v0

--- a/solution.py
+++ b/solution.py
@@ -2,6 +2,7 @@
 import jax.numpy as jnp
 from jax import lax
 from jax.sharding import PartitionSpec as P
+from jax.lax import all_to_all, axis_size
 
 HEADS = 16
 HEAD_DIM = 64
@@ -128,9 +129,21 @@
         )
 
     def feed(settled):
+
+        def report_rounds_up(z, along_axis):
+            return jnp.concatenate(
+                all_to_all(
+                    jnp.stack([z] * axis_size(along_axis), axis=0),
+                    axis_name=along_axis,
+                    split_axis=0,
+                    concat_axis=0,
+                ),
+                axis=1,
+            )
+
         products = jnp.einsum(
             "gtd,df->gtf",
-            lax.all_gather(settled, "tok", axis=1, tiled=True),
+            report_rounds_up(settled, "tok"),
             rows_up,
             preferred_element_type=jnp.float32,
         )

time: 1600 us -> 1490 us (0.931)
  blocking collectives: 459 us -> 290 us
  waiting for transfers between devices: 1000 us -> 1040 us
    all_gather x2 -> x0, blocking collectives: 198 us -> none  [feed(): lax.all_gather(settled, 'tok', axis=1, tiled=True)]
    all_to_all x2, waiting for transfers between devices: 32.7 us -> 66.5 us  [attend(): lax.all_to_all(weighted.reshape(groups, block_len, model_width)[None], 't...]
    all_to_all x0 -> x1, blocking collectives: none -> 28.6 us  [report_rounds_up(): all_to_all(jnp.stack([z] * axis_size(along_axis), axis=0), axis_name=alon...]
  transfers between devices with their start and end apart: 11 -> 12, of which waited for: 11 -> 12; matrix products, arithmetic and copies ran while one was open for 2% -> 2% of each run, Pallas kernels for 0% -> 0%
where the time goes in v1:
time: 1490 us; the launch traced here: 1480 us
  waiting for transfers between devices  1040 us (70%)
  blocking collectives  290 us (19%)
  starting transfers between devices  50.9 us (3%)
  other arithmetic  29.6 us (2%)
  matrix products  28.7 us (2%)
  local copies, waits for them, and re-layouts  23.4 us (2%)
    unnamed x7, waiting for transfers between devices  537 us
    all_gather x2, blocking collectives, feed(): return lax.all_gather(finished, 'tok', axis=1, tiled=True)  197 us
    all_gather x1, waiting for transfers between devices, shards(): lax.all_gather(rows_kv, 'tok', axis=1, tiled=True)  143 us
    all_gather x1, waiting for transfers between devices, shards(): lax.all_gather(rows_q, 'tok', axis=1, tiled=True)  127 us
    all_gather x1, waiting for transfers between devices, shards(): lax.all_gather(rows_o, 'tok', axis=1, tiled=True)  106 us
    all_to_all x2, waiting for transfers between devices, attend(): lax.all_to_all(weighted.reshape(groups, block_len, model_width)[None], 't...  66.5 us
    all_to_all x2, waiting for transfers between devices, attend(): lax.all_to_all(totals[None], 'tok', split_axis=2, concat_axis=0, tiled=True)  31.6 us
    all_to_all x2, waiting for transfers between devices, attend(): lax.all_to_all(peaks[None], 'tok', split_axis=2, concat_axis=0, tiled=True)  30.8 us
  transfers between devices with their start and end apart: 12, of which 12 were waited for; matrix products, arithmetic and copies ran while one was open for 2% of the time, Pallas kernels for 0%

profile of v1, /device:TPU:2, one launch (start us, length us, event | category | flops | bytes accessed | tf_op | source)
XLA Modules:
  0.0 1483.4 jit_solution(6126258030013228949)
XLA Ops:
  6.5 16.2 %all_gather.32 = bf16[1024,16]{0,1:T(8,128)(2,1)} all-gather(bf16[128,16]{0,1:T(8,128)(2,1)} %param.21), channel_id=1, replica_groups=mesh['seq'=8,'tok'=64] {'seq'}, dimensions={0}, use_global_device_ids=true | all-gather | bytes 36864 | tf_op jit(solution)/shard_map/all_gather | solution.py:66
  22.9 13.1 all_gather.30
  38.0 126.6 %all-gather.6.cloned.1.call-done = bf16[1024,1024]{0,1:T(8,128)(2,1)} async-done(((bf16[1024,16]{0,1:T(8,128)(2,1)}), bf16[1024,1024]{0,1:T(8,128)(2,1)}) %all-gather.6.cloned.1.call-update) | async-done | bytes 2097168 | tf_op jit(solution)/shard_map/all_gather | solution.py:73
  167.1 143.0 %all-gather.4.cloned.1.call-done = bf16[1024,2048]{0,1:T(8,128)(2,1)} async-done(((bf16[1024,32]{0,1:T(8,128)(2,1)}), bf16[1024,2048]{0,1:T(8,128)(2,1)}) %all-gather.4.cloned.1.call-update) | async-done | bytes 4194320 | tf_op jit(solution)/shard_map/all_gather | solution.py:74
  310.1 3.4 fusion.32
  314.3 14.3 while.34
  329.3 8.9 all-to-all-start.1
  339.0 15.4 %all-to-all-done.1 = f32[1,1,256,16]{3,1,0,2:T(1,128)S(1)} async-done(((f32[1,1,256,16]{3,1,0,2:T(1,128)}), f32[1,1,256,16]{3,1,0,2:T(1,128)S(1)}, u32[]{:S(2)}, u32[]{:S(2)}) %all-to-all-start.1) | async-done | bytes 16416 | tf_op jit(solution)/shard_map/all_to_all | solution.py:104
  354.4 4.6 all-to-all-start.2
  360.9 14.3 all-to-all-done.2
  375.3 5.5 all-to-all-start
  380.9 12.8 all_gather.34
  398.9 26.6 %all-to-all-done = f32[1,1,256,1024]{3,1,0,2:T(1,128)} async-done(((f32[1,1,256,1024]{3,1,0,2:T(1,128)}), f32[1,1,256,1024]{3,1,0,2:T(1,128)}, u32[]{:S(2)}, u32[]{:S(2)}) %all-to-all-start) | async-done | bytes 1048608 | tf_op jit(solution)/shard_map/all_to_all | solution.py:106
  425.5 3.1 multiply_reduce_fusion.1
  428.6 106.5 %all-gather.8.cloned.1.call-done = bf16[1024,1024]{0,1:T(8,128)(2,1)} async-done(((bf16[1024,16]{0,1:T(8,128)(2,1)}), bf16[1024,1024]{0,1:T(8,128)(2,1)}) %all-gather.8.cloned.1.call-update) | async-done | bytes 2097168 | tf_op jit(solution)/shard_map/all_gather | solution.py:75
  538.7 10.3 all-to-all-start.3
  549.0 11.6 all_gather.36
  560.6 11.0 all_gather.37
  578.2 271.7 %all-reduce.5.cloned.1.call-done = f32[1,256,1024]{2,1,0:T(8,128)} async-done(((f32[1,256,1024]{2,1,0:T(8,128)}), f32[1,256,1024]{2,1,0:T(8,128)}) %all-reduce.5.cloned.1.call-update) | async-done | bytes 1048592
  852.9 98.7 %all_gather.38 = bf16[1,256,1024]{2,0,1:T(2,128)(2,1)S(1)} all-gather(bf16[1,4,1024]{2,0,1:T(2,128)(2,1)S(1)} %copy.77), channel_id=1, replica_groups=mesh['seq'=8,'tok'=64] {'tok'}, dimensions={1}, use_global_device_ids=true | all-gather | bytes 532480 | tf_op jit(solution)/shard_map/all_gather | solution.py:156
  952.9 3.4 fusion.33
  957.0 14.5 while.35
  972.3 10.6 all-to-all-start.5
  983.7 15.4 %all-to-all-done.5 = f32[1,1,256,16]{3,1,0,2:T(1,128)S(1)} async-done(((f32[1,1,256,16]{3,1,0,2:T(1,128)}), f32[1,1,256,16]{3,1,0,2:T(1,128)S(1)}, u32[]{:S(2)}, u32[]{:S(2)}) %all-to-all-start.5) | async-done | bytes 16416 | tf_op jit(solution)/shard_map/all_to_all | solution.py:104
  999.1 4.6 all-to-all-start.6
  1005.7 17.2 %all-to-all-done.6 = f32[1,1,256,16]{3,1,0,2:T(1,128)S(1)} async-done(((f32[1,1,256,16]{3,1,0,2:T(1,128)}), f32[1,1,256,16]{3,1,0,2:T(1,128)S(1)}, u32[]{:S(2)}, u32[]{:S(2)}) %all-to-all-start.6) | async-done | bytes 16416 | tf_op jit(solution)/shard_map/all_to_all | solution.py:105
  1022.9 6.0 all-to-all-start.4
  1034.4 39.8 %all-to-all-done.4 = f32[1,1,256,1024]{3,1,0,2:T(1,128)} async-done(((f32[1,1,256,1024]{3,1,0,2:T(1,128)}), f32[1,1,256,1024]{3,1,0,2:T(1,128)}, u32[]{:S(2)}, u32[]{:S(2)}) %all-to-all-start.4) | async-done | bytes 1048608 | tf_op jit(solution)/shard_map/all_to_all | solution.py:106
  1074.2 3.1 multiply_reduce_fusion
  1079.2 28.6 %all_to_all.88 = bf16[64,1,4,1024]{3,2,1,0:T(4,128)(2,1)S(1)} all-to-all(bf16[64,1,4,1024]{3,2,1,0:T(4,128)(2,1)S(1)} %stack.7), channel_id=1, replica_groups=mesh['seq'=8,'tok'=64] {'tok'}, dimensions={0} | all-to-all | bytes 1048576 | tf_op jit(solution)/shard_map/all_to_all | solution.py:135
  1110.1 265.0 %all-reduce.7.cloned.1.call-done = f32[1,256,1024]{2,1,0:T(8,128)} async-done(((f32[1,256,1024]{2,1,0:T(8,128)}), f32[1,256,1024]{2,1,0:T(8,128)}) %all-reduce.7.cloned.1.call-update) | async-done | bytes 1048592
  1377.8 98.1 %all_gather.39 = bf16[1,256,1024]{2,0,1:T(2,128)(2,1)S(1)} all-gather(bf16[1,4,1024]{2,0,1:T(2,128)(2,1)S(1)} %copy.87), channel_id=1, replica_groups=mesh['seq'=8,'tok'=64] {'tok'}, dimensions={1}, use_global_device_ids=true | all-gather | bytes 532480 | tf_op jit(solution)/shard_map/all_gather | solution.py:156
  (168 shorter events, 69.9 us)
Async XLA Ops:
  6.5 158.0 %copy-start.3 = (bf16[1,256,1024]{2,1,0:T(8,128)(2,1)S(1)}, bf16[1,256,1024]{2,1,0:T(8,128)(2,1)}, u32[]{:S(2)}) copy-start(bf16[1,256,1024]{2,1,0:T(8,128)(2,1)} %param.16) | copy-start | bytes 1572868
  6.5 158.0 %all-gather.6.cloned.1.call-start = ((), (), s32[]{:S(2)}) async-start(), calls=%async_computation.9 | async-start | bytes 2129920 | tf_op jit(solution)/shard_map/all_gather | solution.py:73
  22.8 287.3 %all-gather.4.cloned.1.call-start = ((), (), s32[]{:S(2)}) async-start(), calls=%async_computation.8 | async-start | bytes 4259840 | tf_op jit(solution)/shard_map/all_gather | solution.py:74
  167.1 147.2 %copy-start.6 = (s32[1,3]{1,0:T(1,128)S(1)}, s32[1,3]{1,0:T(1,128)}, u32[]{:S(2)}) copy-start(s32[1,3]{1,0:T(1,128)} %param.19) | copy-start | bytes 40
  329.3 25.0 %all-to-all-start.1 = ((f32[1,1,256,16]{3,1,0,2:T(1,128)}), f32[1,1,256,16]{3,1,0,2:T(1,128)S(1)}, u32[]{:S(2)}, u32[]{:S(2)}) async-start(f32[1,1,256,16]{3,1,0,2:T(1,128)} %bitcast.47), calls=%async_computation.1 | async-start | bytes 262144 | tf_op jit(solution)/shard_map/all_to_all | solution.py:104
  354.4 20.9 %all-to-all-start.2 = ((f32[1,1,256,16]{3,1,0,2:T(1,128)}), f32[1,1,256,16]{3,1,0,2:T(1,128)S(1)}, u32[]{:S(2)}, u32[]{:S(2)}) async-start(f32[1,1,256,16]{3,1,0,2:T(1,128)} %bitcast.49), calls=%async_computation.2 | async-start | bytes 262144 | tf_op jit(solution)/shard_map/all_to_all | solution.py:105
  359.0 21.9 %copy-start.10 = (bf16[128,16]{0,1:T(8,128)(2,1)S(1)}, bf16[128,16]{0,1:T(8,128)(2,1)}, u32[]{:S(2)}) copy-start(bf16[128,16]{0,1:T(8,128)(2,1)} %param.23) | copy-start | bytes 12292
  375.3 50.2 %all-to-all-start = ((f32[1,1,256,1024]{3,1,0,2:T(1,128)}), f32[1,1,256,1024]{3,1,0,2:T(1,128)}, u32[]{:S(2)}, u32[]{:S(2)}) async-start(f32[1,1,256,1024]{3,1,0,2:T(1,128)} %copy.74), calls=%async_computation | async-start | bytes 2097152 | tf_op jit(solution)/shard_map/all_to_all | solution.py:106
  380.8 154.3 %all-gather.8.cloned.1.call-start = ((), (), s32[]{:S(2)}) async-start(), calls=%async_computation.10 | async-start | bytes 2129920 | tf_op jit(solution)/shard_map/all_gather | solution.py:75
  396.1 139.0 %copy-start.4 = (bf16[1,256,1024]{2,1,0:T(8,128)(2,1)S(1)}, bf16[1,256,1024]{2,1,0:T(8,128)(2,1)}, u32[]{:S(2)}) copy-start(bf16[1,256,1024]{2,1,0:T(8,128)(2,1)} %param.16) | copy-start | bytes 1572868
  425.5 112.2 %copy-start.5 = (f32[1024]{0:T(1024)S(1)}, f32[1024]{0:T(1024)}, u32[]{:S(2)}) copy-start(f32[1024]{0:T(1024)} %param.24) | copy-start | bytes 12292
  428.6 120.4 %copy-start.7 = (bf16[128,64]{0,1:T(8,128)(2,1)S(1)}, bf16[128,64]{0,1:T(8,128)(2,1)}, u32[]{:S(2)}) copy-start(bf16[128,64]{0,1:T(8,128)(2,1)} %param.25) | copy-start | bytes 49156
  428.6 132.0 %copy-start.8 = (bf16[64,128]{1,0:T(8,128)(2,1)S(1)}, bf16[64,128]{1,0:T(8,128)(2,1)}, u32[]{:S(2)}) copy-start(bf16[64,128]{1,0:T(8,128)(2,1)} %param.26) | copy-start | bytes 49156
  538.7 33.6 %all-to-all-start.3 = ((bf16[64,1,4,1024]{3,2,1,0:T(4,128)(2,1)}), bf16[64,1,4,1024]{3,2,1,0:T(4,128)(2,1)S(1)}, u32[]{:S(2)}, u32[]{:S(2)}) async-start(bf16[64,1,4,1024]{3,2,1,0:T(4,128)(2,1)} %stack.6), calls=%async_computation.3 | async-start | bytes 1048576 | tf_op jit(solution)/shard_map/all_to_all | solution.py:135
  548.9 301.0 %all-reduce.5.cloned.1.call-start = ((), (), s32[]{:S(2)}) async-start(), calls=%async_computation.11 | async-start | bytes 2097152
  571.6 6.5 copy-start.11
  571.6 280.4 %copy-start.9 = (f32[1024]{0:T(1024)S(1)}, f32[1024]{0:T(1024)}, u32[]{:S(2)}) copy-start(f32[1024]{0:T(1024)} %param.27) | copy-start | bytes 12292
  849.9 101.9 %copy-start.12 = (bf16[1024,1024]{0,1:T(8,128)(2,1)S(1)}, bf16[1024,1024]{0,1:T(8,128)(2,1)}, u32[]{:S(2)}) copy-start(bf16[1024,1024]{0,1:T(8,128)(2,1)} %all-gather.6.cloned.1.call-done) | copy-start | bytes 6291460
  951.8 1.0 copy-start.1
  972.3 26.8 %all-to-all-start.5 = ((f32[1,1,256,16]{3,1,0,2:T(1,128)}), f32[1,1,256,16]{3,1,0,2:T(1,128)S(1)}, u32[]{:S(2)}, u32[]{:S(2)}) async-start(f32[1,1,256,16]{3,1,0,2:T(1,128)} %bitcast.69), calls=%async_computation.5 | async-start | bytes 262144 | tf_op jit(solution)/shard_map/all_to_all | solution.py:104
  999.1 23.8 %all-to-all-start.6 = ((f32[1,1,256,16]{3,1,0,2:T(1,128)}), f32[1,1,256,16]{3,1,0,2:T(1,128)S(1)}, u32[]{:S(2)}, u32[]{:S(2)}) async-start(f32[1,1,256,16]{3,1,0,2:T(1,128)} %bitcast.71), calls=%async_computation.6 | async-start | bytes 262144 | tf_op jit(solution)/shard_map/all_to_all | solution.py:105
  1022.9 51.3 %all-to-all-start.4 = ((f32[1,1,256,1024]{3,1,0,2:T(1,128)}), f32[1,1,256,1024]{3,1,0,2:T(1,128)}, u32[]{:S(2)}, u32[]{:S(2)}) async-start(f32[1,1,256,1024]{3,1,0,2:T(1,128)} %copy.84), calls=%async_computation.4 | async-start | bytes 2097152 | tf_op jit(solution)/shard_map/all_to_all | solution.py:106
  1028.9 346.1 %all-reduce.7.cloned.1.call-start = ((), (), s32[]{:S(2)}) async-start(), calls=%async_computation.12 | async-start | bytes 2097152
  1031.5 45.8 %copy-start = (bf16[1024,1024]{0,1:T(8,128)(2,1)S(1)}, bf16[1024,1024]{0,1:T(8,128)(2,1)}, u32[]{:S(2)}) copy-start(bf16[1024,1024]{0,1:T(8,128)(2,1)} %all-gather.8.cloned.1.call-done) | copy-start | bytes 6291460
  1108.0 367.9 %copy-start.2 = (bf16[1,256,1024]{2,1,0:T(8,128)(2,1)S(1)}, bf16[1,256,1024]{2,1,0:T(8,128)(2,1)}, u32[]{:S(2)}) copy-start(bf16[1,256,1024]{2,1,0:T(8,128)(2,1)} %copy-done.1) | copy-start | bytes 1572868
Sparse Core Ops, SparseCore 0:
  22.9 141.5 all-gather.5
  167.5 142.5 all-gather.3
  393.9 141.1 all-gather.7
  576.3 273.5 all-reduce.4
  1110.2 264.7 all-reduce.6
